TPU v7x, 32 devices: a whole 2x2x4 slice. The times are simulated.
32 devices in a mesh: space: 8 (over y, x, core), src: 4 (over z).
Axes of the slice: x: 2, y: 2, z: 4, core: 2. Of those that a mesh axis runs over, the one named last changes fastest.
Arguments:
- potential_start: float32 [16, 4, 128, 1024], P('src', None, 'space'), may hold values from -6 to 6
- adjoint_start: float32 [16, 4, 128, 1024], P('src', None, 'space'), may hold values from -6 to 6
- conductivity: float32 [4, 128, 1024], P(None, 'space', 'src'), may hold values from 0.1 to 1
- electrodes: int32 [16, 2], P('src'), may hold values from 0 to 131071
- receivers: int32 [16, 32, 2], P('src'), may hold values from 0 to 131071
- observed: float32 [16, 32], P('src'), may hold values from -6 to 6
Outputs:
- gradient: float32 [4, 128, 1024], P(None, 'space', 'src')
Inputs may be any that keep to these rules, and one draw needn't show every extreme that they name: `electrodes`: each entry is a surface node id row * 1024 + column. `receivers`: each entry is a surface node id row * 1024 + column.
All inputs are finite; a program needn't handle non-finite values.
Results may differ from a plain program's by a relative error of at most 0.00002.
Values sent between devices are 32-bit elements; how exact they have to be, the bound alone decides.
No kernel may reach another device: no remote copies, remote signals or barrier semaphores. Data moves between devices by JAX's collectives and lax.ppermute only.
A program may use at most 64 MiB of HBM per device.

v0:
```python
import jax
import jax.numpy as jnp
from jax import lax
from jax.sharding import PartitionSpec as P

SWEEPS = 4
GAMMA = 0.5
CURRENT = 4.0
THETA = 1.025
DELTA = 0.975
RATIO = THETA / DELTA


def padded_2(block, sides, width):
    for axis, dim in sides:
        count = lax.axis_size(axis)
        forward = [(i, i + 1) for i in range(count - 1)]
        backward = [(target, source) for source, target in forward]
        low = lax.ppermute(
            lax.slice_in_dim(block, block.shape[dim] - width, None, axis=dim), axis, forward
        )
        high = lax.ppermute(lax.slice_in_dim(block, 0, width, axis=dim), axis, backward)
        block = jnp.concatenate([low, block, high], axis=dim)
    return block


def pad_axis(field, dimension, margin):
    widths = [(0, 0)] * field.ndim
    widths[dimension % field.ndim] = (margin, margin)
    return jnp.pad(field, widths)


def coefficients(padded_sigma):
    centre_sigma = padded_sigma[:, 1:-1, :]
    layer_pad = pad_axis(centre_sigma, 0, 1)
    column_pad = pad_axis(centre_sigma, 2, 1)
    face_terms = (
        0.5 * (centre_sigma + padded_sigma[:, :-2, :]),
        0.5 * (centre_sigma + padded_sigma[:, 2:, :]),
        0.5 * (centre_sigma + column_pad[:, :, :-2]),
        0.5 * (centre_sigma + column_pad[:, :, 2:]),
        0.5 * (centre_sigma + layer_pad[:-2]),
        0.5 * (centre_sigma + layer_pad[2:]),
    )
    diagonal = (
        face_terms[0]
        + face_terms[1]
        + face_terms[2]
        + face_terms[3]
        + face_terms[4]
        + face_terms[5]
        + GAMMA * centre_sigma
    )
    return (face_terms, diagonal)


def apply_operator(padded, face_terms, diagonal):
    centre = padded[..., 1:-1, :]
    layer_pad = pad_axis(centre, -3, 1)
    column_pad = pad_axis(centre, -1, 1)
    neighbours = (
        face_terms[0] * padded[..., :-2, :]
        + face_terms[1] * padded[..., 2:, :]
        + face_terms[2] * column_pad[..., :-2]
        + face_terms[3] * column_pad[..., 2:]
        + face_terms[4] * layer_pad[..., :-2, :, :]
        + face_terms[5] * layer_pad[..., 2:, :, :]
    )
    return diagonal * centre - neighbours


def chebyshev(initial, source, face_terms, diagonal, inverse, extend, inside_rows):
    residual = source - apply_operator(extend(initial), face_terms, diagonal)
    residual = residual * inside_rows
    direction = inverse * residual / THETA
    factor = 1.0 / RATIO
    potential = initial
    for sweep in range(SWEEPS):
        potential = potential + direction
        if sweep + 1 < SWEEPS:
            residual = residual - apply_operator(extend(direction), face_terms, diagonal)
            residual = residual * inside_rows
            factor_next = 1.0 / (2.0 * RATIO - factor)
            direction = (
                factor_next * factor * direction + 2.0 * factor_next / DELTA * inverse * residual
            )
            factor = factor_next
    return potential


def sensitivity(forward_pad, adjoint_pad):
    forward_mid = forward_pad[..., 1:-1, :]
    adjoint_mid = adjoint_pad[..., 1:-1, :]
    forward_layer = pad_axis(forward_mid, -3, 1)
    adjoint_layer = pad_axis(adjoint_mid, -3, 1)
    forward_column = pad_axis(forward_mid, -1, 1)
    adjoint_column = pad_axis(adjoint_mid, -1, 1)
    pairs = (
        (forward_pad[..., :-2, :], adjoint_pad[..., :-2, :]),
        (forward_pad[..., 2:, :], adjoint_pad[..., 2:, :]),
        (forward_column[..., :-2], adjoint_column[..., :-2]),
        (forward_column[..., 2:], adjoint_column[..., 2:]),
        (forward_layer[..., :-2, :, :], adjoint_layer[..., :-2, :, :]),
        (forward_layer[..., 2:, :, :], adjoint_layer[..., 2:, :, :]),
    )
    running = GAMMA * forward_mid * adjoint_mid
    for forward_near, adjoint_near in pairs:
        running = running + 0.5 * (forward_mid - forward_near) * (adjoint_mid - adjoint_near)
    return -running


def local_pad(field):
    return pad_axis(field, -2, 1)


def surface_source(node_ids, amounts, base_row, span, layer_count, columns):
    sources_here = node_ids.shape[0]
    local_ids = node_ids - base_row * columns
    inside = (local_ids >= 0) & (local_ids < span * columns)
    slots = jnp.clip(local_ids, 0, span * columns - 1)
    source_rows = jnp.broadcast_to(
        jnp.arange(sources_here, dtype=jnp.int32)[:, None], node_ids.shape
    )
    plane = (
        jnp.zeros((sources_here, span * columns), jnp.float32)
        .at[source_rows, slots]
        .add(jnp.where(inside, amounts, 0.0))
    )
    plane = plane.reshape(sources_here, 1, span, columns)
    return jnp.concatenate(
        [plane, jnp.zeros((sources_here, layer_count - 1, span, columns), jnp.float32)], axis=1
    )


def per_device(potential_start, adjoint_start, conductivity, electrodes, receivers, observed):
    sources_here, layer_count, row_count, columns = potential_start.shape
    whole_sigma = lax.all_gather(conductivity, "src", axis=2, tiled=True)
    first_row = lax.axis_index("space") * row_count
    total_rows = row_count * lax.axis_size("space")
    margin_rows = SWEEPS + 1

    def widen(field):
        return padded_2(field, (("space", 2),), margin_rows)

    padded_sigma = padded_2(whole_sigma, (("space", 1),), margin_rows + 1)
    face_terms, diagonal = coefficients(padded_sigma)
    global_rows = first_row - margin_rows + jnp.arange(row_count + 2 * margin_rows, dtype=jnp.int32)
    inside_rows = ((global_rows >= 0) & (global_rows < total_rows)).astype(jnp.float32)[:, None]
    inverse = 1.0 / jnp.where(inside_rows > 0, diagonal, 1.0)
    forward_init = widen(potential_start)
    adjoint_init = widen(adjoint_start)
    span = row_count + 2 * margin_rows
    base_row = first_row - margin_rows
    currents = jnp.broadcast_to(jnp.array([CURRENT, -CURRENT], jnp.float32), electrodes.shape)
    injected = surface_source(electrodes, currents, base_row, span, layer_count, columns)
    forward = chebyshev(
        forward_init, injected, face_terms, diagonal, inverse, local_pad, inside_rows
    )
    surface = forward[:, 0, margin_rows : margin_rows + row_count, :].reshape(
        sources_here, row_count * columns
    )

    def read_nodes(node_ids):
        local_ids = node_ids - first_row * columns
        inside = (local_ids >= 0) & (local_ids < row_count * columns)
        picked = jnp.take_along_axis(
            surface, jnp.clip(local_ids, 0, row_count * columns - 1), axis=1
        )
        return jnp.where(inside, picked, 0.0)

    local_readings = read_nodes(receivers[:, :, 0]) - read_nodes(receivers[:, :, 1])
    predicted = lax.psum(local_readings, "space")
    misfit = predicted - observed
    adjoint_source = surface_source(
        jnp.concatenate([receivers[:, :, 0], receivers[:, :, 1]], axis=1),
        jnp.concatenate([misfit, -misfit], axis=1),
        base_row,
        span,
        layer_count,
        columns,
    )
    adjoint = chebyshev(
        adjoint_init, adjoint_source, face_terms, diagonal, inverse, local_pad, inside_rows
    )
    forward_pad = forward[:, :, margin_rows - 1 : margin_rows + row_count + 1, :]
    adjoint_pad = adjoint[:, :, margin_rows - 1 : margin_rows + row_count + 1, :]
    local_terms = jnp.sum(sensitivity(forward_pad, adjoint_pad), axis=0)
    summed = lax.psum(local_terms, "src")
    share = columns // lax.axis_size("src")
    return lax.dynamic_slice_in_dim(summed, lax.axis_index("src") * share, share, 2)


def solution(mesh):
    return jax.shard_map(
        per_device,
        mesh=mesh,
        in_specs=(
            P("src", None, "space", None),
            P("src", None, "space", None),
            P(None, "space", "src"),
            P("src", None),
            P("src", None, None),
            P("src", None),
        ),
        out_specs=P(None, "space", "src"),
        check_vma=False,
    )
```

profile of v0, /device:TPU:0, one launch (start us, length us, event | category | flops | bytes accessed | tf_op | source)
XLA Modules:
  0.0 187.9 jit_solution(12918429776498886450)
XLA Ops:
  6.5 16.0 %all_gather.3 = f32[4,16,1024]{2,1,0:T(8,128)S(1)} all-gather(f32[4,16,256]{2,1,0:T(8,128)} %param.11), channel_id=1, replica_groups=mesh['space'=8,'src'=4] {'src'}, dimensions={2}, use_global_device_ids=true | all-gather | bytes 327680 | tf_op jit(solution)/shard_map/all_gather | solution.py:137
  22.6 1.3 collective-permute-start.2
  25.2 2.3 %fusion.150 = (f32[4,4,5,1024]{3,2,0,1:T(8,128)}, f32[4,4,5,1024]{3,2,0,1:T(8,128)}) fusion(f32[4,4,16,1024]{3,2,1,0:T(8,128)} %param.9), kind=kLoop, calls=%fused_computation.233 | loop fusion | bytes 1703936 | tf_op jit(solution)/shard_map/slice | solution.py:20
  27.5 5.6 %collective-permute-start = (f32[4,4,5,1024]{3,2,0,1:T(8,128)}, f32[4,4,5,1024]{3,2,0,1:T(8,128)}, u32[]{:S(2)}, u32[]{:S(2)}) collective-permute-start(f32[4,4,5,1024]{3,2,0,1:T(8,128)} %get-tuple-element.28), channel_id=1, source_target_pairs={{0,4},{4,8},{8,12},{12,16},{16,20},{20,24},{24,28},{1,5},{5,9},{9,... | collective-permute-start | bytes 983048 | tf_op jit(solution)/shard_map/ppermute | solution.py:19
  35.5 4.3 %collective-permute-start.4 = (f32[4,4,5,1024]{3,2,0,1:T(8,128)}, f32[4,4,5,1024]{3,2,0,1:T(8,128)}, u32[]{:S(2)}, u32[]{:S(2)}) collective-permute-start(f32[4,4,5,1024]{3,2,0,1:T(8,128)} %get-tuple-element.26), channel_id=1, source_target_pairs={{0,4},{4,8},{8,12},{12,16},{16,20},{20,24},{24,28},{1,5},{5,9},{9,... | collective-permute-start | bytes 983048 | tf_op jit(solution)/shard_map/ppermute | solution.py:19
  46.1 2.2 %pad_maximum_fusion = f32[4,4,26,1024]{3,2,0,1:T(8,128)S(1)} fusion(f32[4,4,5,1024]{3,2,0,1:T(8,128)} %collective-permute-done.1, f32[4,4,5,1024]{3,2,0,1:T(8,128)} %collective-permute-done, f32[4,4,16,1024]{3,2,1,0:T(8,128)S(1)} %copy-done.8), kind=kLoop, calls=%fused_computation.130 | loop fusion | flops 851968 | bytes 3407872 | tf_op jit(solution)/shard_map/concatenate | solution.py:23
  48.3 2.6 %multiply_multiply_fusion.1 = (f32[4,4,26,1024]{3,2,0,1:T(8,128)S(1)}, f32[4,4,26,1024]{3,2,0,1:T(8,128)S(1)}) fusion(f32[4,26,1024]{2,1,0:T(8,128)S(1)} %get-tuple-element.15, f32[26]{0:T(128)S(1)} %and_convert_fusion, f32[4,26,1024]{2,1,0:T(8,128)S(1)} %get-tuple-element.31, f32[4,4,26,1024]{3,2,0,1:T(8,128)S(1)} %pad_maximum_fusion, ...), kind=kLoop, calls=%fused_computation.137 | loop fusion | flops 7241728 | bytes 8945768 | tf_op jit(solution)/shard_map/div | solution.py:75
  50.9 2.8 %multiply_add_fusion.3 = (f32[4,4,26,1024]{3,2,0,1:T(8,128)S(1)}, f32[4,4,26,1024]{3,2,0,1:T(8,128)S(1)}) fusion(f32[4,4,26,1024]{3,2,0,1:T(8,128)S(1)} %get-tuple-element.23, f32[4,26,1024]{2,1,0:T(8,128)S(1)} %get-tuple-element.41, f32[4,26,1024]{2,1,0:T(8,128)S(1)} %get-tuple-element.15, f32[26]{0:T(128)S(1)} %and_convert_fusion, ...), kind=kLoop, calls=%fused_computation.135 | loop fusion | flops 8093696 | bytes 10649704 | tf_op jit(solution)/shard_map/add | solution.py:85
  53.7 3.1 %multiply_add_fusion.2 = (f32[4,4,26,1024]{3,2,0,1:T(8,128)S(1)}, f32[4,4,26,1024]{3,2,0,1:T(8,128)S(1)}) fusion(f32[4,26,1024]{2,1,0:T(8,128)S(1)} %get-tuple-element.40, f32[4,4,26,1024]{3,2,0,1:T(8,128)S(1)} %get-tuple-element.21, f32[4,26,1024]{2,1,0:T(8,128)S(1)} %get-tuple-element.41, f32[4,4,26,1024]{3,2,0,1:T(8,128)S(1)} %get-tuple-element.23, ...), kind=kLoop, calls=%fused_computation.134 | loop fusion | flops 9371648 | bytes 12779624 | tf_op jit(solution)/shard_map/add | solution.py:85
  56.9 4.9 %fusion.37 = f32[4,4,26,1024]{3,2,0,1:T(8,128)S(1)} fusion(f32[4,4,26,1024]{3,2,0,1:T(8,128)S(1)} %get-tuple-element.19, f32[4,4,26,1024]{3,2,0,1:T(8,128)S(1)} %get-tuple-element.18, f32[4,4,26,1024]{3,2,0,1:T(8,128)S(1)} %get-tuple-element.23, f32[4,26,1024]{2,1,0:T(8,128)S(1)} %get-tuple-element.14, f32[26]{0:T(128)S(1)} %and_convert_fusion, ...), kind=kLoop, calls=%fused_computation.73 | loop fusion | flops 12353536 | bytes 14483560 | tf_op jit(solution)/shard_map/add | solution.py:79
  64.5 1.5 gather_fusion
  66.1 1.5 gather_fusion.1
  67.8 16.1 %psum.14 = f32[4,32]{1,0:T(4,128)S(1)} all-reduce(f32[4,32]{1,0:T(4,128)S(1)} %fusion.136), channel_id=1, replica_groups=mesh['space'=8,'src'=4] {'space'}, use_global_device_ids=true, to_apply=%region_1.3 | all-reduce | flops 128 | bytes 1024 | tf_op jit(solution)/shard_map/psum | solution.py:172
  84.9 35.8 %scatter_fusion.1 = f32[4,26624]{1,0:T(4,128)} fusion(f32[4,26624]{1,0:T(4,128)} %broadcast.247, s32[256]{0:T(256)S(1)} %reshape.118, f32[256]{0:T(256)S(1)} %reshape.120), kind=kCustom, calls=%fused_computation.3 | custom fusion | flops 256 | bytes 5120 | tf_op jit(solution)/shard_map/scatter-add | solution.py:127
  120.7 2.2 %reshape.98 = f32[4,1,26,1024]{3,2,0,1:T(8,128)} reshape(f32[4,26624]{1,0:T(4,128)} %scatter_fusion.1) | data formatting | bytes 851968 | tf_op jit(solution)/shard_map/reshape | solution.py:129
  122.9 2.0 %pad_maximum_fusion.1 = f32[4,4,26,1024]{3,2,0,1:T(8,128)S(1)} fusion(f32[4,4,5,1024]{3,2,0,1:T(8,128)} %collective-permute-done.5, f32[4,4,5,1024]{3,2,0,1:T(8,128)} %collective-permute-done.4, f32[4,4,16,1024]{3,2,1,0:T(8,128)} %param.10), kind=kLoop, calls=%fused_computation.131 | loop fusion | flops 851968 | bytes 3407872 | tf_op jit(solution)/shard_map/concatenate | solution.py:23
  124.9 2.6 %multiply_multiply_fusion = (f32[4,4,26,1024]{3,2,0,1:T(8,128)S(1)}, f32[4,4,26,1024]{3,2,0,1:T(8,128)S(1)}) fusion(f32[4,26,1024]{2,1,0:T(8,128)S(1)} %get-tuple-element.15, f32[26]{0:T(128)S(1)} %and_convert_fusion, f32[4,26,1024]{2,1,0:T(8,128)S(1)} %get-tuple-element.31, f32[4,4,26,1024]{3,2,0,1:T(8,128)S(1)} %pad_maximum_fusion.1, ...), kind=kLoop, calls=%fused_computation.136 | loop fusion | flops 7241728 | bytes 8945768 | tf_op jit(solution)/shard_map/div | solution.py:75
  127.5 2.8 %multiply_add_fusion.1 = (f32[4,4,26,1024]{3,2,0,1:T(8,128)S(1)}, f32[4,4,26,1024]{3,2,0,1:T(8,128)S(1)}) fusion(f32[4,4,26,1024]{3,2,0,1:T(8,128)S(1)} %get-tuple-element.11, f32[4,26,1024]{2,1,0:T(8,128)S(1)} %copy-done.5, f32[4,26,1024]{2,1,0:T(8,128)S(1)} %get-tuple-element.15, f32[26]{0:T(128)S(1)} %and_convert_fusion, ...), kind=kLoop, calls=%fused_computation.133 | loop fusion | flops 8093696 | bytes 10649704 | tf_op jit(solution)/shard_map/add | solution.py:85
  130.3 3.1 %multiply_add_fusion = (f32[4,4,26,1024]{3,2,0,1:T(8,128)S(1)}, f32[4,4,26,1024]{3,2,0,1:T(8,128)S(1)}) fusion(f32[4,26,1024]{2,1,0:T(8,128)S(1)} %copy-done.14, f32[4,4,26,1024]{3,2,0,1:T(8,128)S(1)} %get-tuple-element.9, f32[4,26,1024]{2,1,0:T(8,128)S(1)} %copy-done.5, f32[4,4,26,1024]{3,2,0,1:T(8,128)S(1)} %get-tuple-element.11, ...), kind=kLoop, calls=%fused_computation.132 | loop fusion | flops 9371648 | bytes 12779624 | tf_op jit(solution)/shard_map/add | solution.py:85
  133.5 5.0 %fusion.76 = f32[4,4,26,1024]{3,2,0,1:T(8,128)S(1)} fusion(f32[4,4,26,1024]{3,2,0,1:T(8,128)S(1)} %get-tuple-element.7, f32[4,4,26,1024]{3,2,0,1:T(8,128)S(1)} %get-tuple-element.6, f32[4,4,26,1024]{3,2,0,1:T(8,128)S(1)} %get-tuple-element.11, f32[4,26,1024]{2,1,0:T(8,128)S(1)} %copy-done.12, f32[26]{0:T(128)S(1)} %and_convert_fusion, ...), kind=kLoop, calls=%fused_computation.112 | loop fusion | flops 12353536 | bytes 14483560 | tf_op jit(solution)/shard_map/add | solution.py:79
  138.7 1.4 copy-done.7
  140.1 1.8 fusion.101
  142.7 36.9 %all-reduce.34.cloned.1.call-done = f32[4,16,1024]{2,1,0:T(8,128)} async-done(((f32[4,16,1024]{2,1,0:T(8,128)}), f32[4,16,1024]{2,1,0:T(8,128)}) %all-reduce.34.cloned.1.call-update) | async-done | bytes 262160 | tf_op jit(solution)/shard_map/psum | solution.py:188
  179.6 1.5 constant_dynamic-slice_fusion
  (93 shorter events, 14.6 us)
Async XLA Ops:
  6.5 27.8 %copy-start.9 = (f32[4,4,16,1024]{3,2,1,0:T(8,128)S(1)}, f32[4,4,16,1024]{3,2,1,0:T(8,128)}, u32[]{:S(2)}) copy-start(f32[4,4,16,1024]{3,2,1,0:T(8,128)} %param.10) | copy-start | bytes 3145732
  6.5 173.1 %all-reduce.34.cloned.1.call-start = ((), (), s32[]{:S(2)}) async-start(), calls=%async_computation | async-start | bytes 524288 | tf_op jit(solution)/shard_map/psum | solution.py:188
  22.6 20.1 %collective-permute-start.2 = (f32[4,6,1024]{2,1,0:T(8,128)S(1)}, f32[4,6,1024]{2,1,0:T(8,128)S(1)}, u32[]{:S(2)}, u32[]{:S(2)}) collective-permute-start(f32[4,6,1024]{2,1,0:T(8,128)S(1)} %get-tuple-element.36), channel_id=1, source_target_pairs={{0,4},{4,8},{8,12},{12,16},{16,20},{20,24},{24,28},{1,5},{5,9},{9,... | collective-permute-start | bytes 294920 | tf_op jit(solution)/shard_map/ppermute | solution.py:19
  23.9 15.9 %copy-start.20 = (s32[4,2]{0,1:T(2,128)S(1)}, s32[4,2]{0,1:T(2,128)}, u32[]{:S(2)}) copy-start(s32[4,2]{0,1:T(2,128)} %param.12) | copy-start | bytes 100
  23.9 16.1 %copy-start.23 = (f32[2]{0:T(128)S(1)}, f32[2]{0:T(128)}, u32[]{:S(2)}) copy-start(f32[2]{0:T(128)} %constant.30.clone) | copy-start | bytes 28
  23.9 20.1 %collective-permute-start.3 = (f32[4,6,1024]{2,1,0:T(8,128)S(1)}, f32[4,6,1024]{2,1,0:T(8,128)S(1)}, u32[]{:S(2)}, u32[]{:S(2)}) collective-permute-start(f32[4,6,1024]{2,1,0:T(8,128)S(1)} %get-tuple-element.37), channel_id=1, source_target_pairs={{4,0},{8,4},{12,8},{16,12},{20,16},{24,20},{28,24},{5,1},{9,5},{13... | collective-permute-start | bytes 294920 | tf_op jit(solution)/shard_map/ppermute | solution.py:22
  27.5 18.2 %collective-permute-start = (f32[4,4,5,1024]{3,2,0,1:T(8,128)}, f32[4,4,5,1024]{3,2,0,1:T(8,128)}, u32[]{:S(2)}, u32[]{:S(2)}) collective-permute-start(f32[4,4,5,1024]{3,2,0,1:T(8,128)} %get-tuple-element.28), channel_id=1, source_target_pairs={{0,4},{4,8},{8,12},{12,16},{16,20},{20,24},{24,28},{1,5},{5,9},{9,... | collective-permute-start | bytes 983048 | tf_op jit(solution)/shard_map/ppermute | solution.py:19
  33.1 12.6 %collective-permute-start.1 = (f32[4,4,5,1024]{3,2,0,1:T(8,128)}, f32[4,4,5,1024]{3,2,0,1:T(8,128)}, u32[]{:S(2)}, u32[]{:S(2)}) collective-permute-start(f32[4,4,5,1024]{3,2,0,1:T(8,128)} %get-tuple-element.29), channel_id=1, source_target_pairs={{4,0},{8,4},{12,8},{16,12},{20,16},{24,20},{28,24},{5,1},{9,5},{13... | collective-permute-start | bytes 983048 | tf_op jit(solution)/shard_map/ppermute | solution.py:22
  35.5 87.4 %collective-permute-start.4 = (f32[4,4,5,1024]{3,2,0,1:T(8,128)}, f32[4,4,5,1024]{3,2,0,1:T(8,128)}, u32[]{:S(2)}, u32[]{:S(2)}) collective-permute-start(f32[4,4,5,1024]{3,2,0,1:T(8,128)} %get-tuple-element.26), channel_id=1, source_target_pairs={{0,4},{4,8},{8,12},{12,16},{16,20},{20,24},{24,28},{1,5},{5,9},{9,... | collective-permute-start | bytes 983048 | tf_op jit(solution)/shard_map/ppermute | solution.py:19
  42.6 80.2 %collective-permute-start.5 = (f32[4,4,5,1024]{3,2,0,1:T(8,128)}, f32[4,4,5,1024]{3,2,0,1:T(8,128)}, u32[]{:S(2)}, u32[]{:S(2)}) collective-permute-start(f32[4,4,5,1024]{3,2,0,1:T(8,128)} %get-tuple-element.27), channel_id=1, source_target_pairs={{4,0},{8,4},{12,8},{16,12},{20,16},{24,20},{28,24},{5,1},{9,5},{13... | collective-permute-start | bytes 983048 | tf_op jit(solution)/shard_map/ppermute | solution.py:22
  44.6 12.2 %copy-start.11 = (f32[4,26,1024]{2,1,0:T(8,128)}, f32[4,26,1024]{2,1,0:T(8,128)S(1)}, u32[]{:S(2)}) copy-start(f32[4,26,1024]{2,1,0:T(8,128)S(1)} %get-tuple-element.14) | copy-start | bytes 1277956
  45.6 5.3 %copy-start.15 = (f32[4,26,1024]{2,1,0:T(8,128)}, f32[4,26,1024]{2,1,0:T(8,128)S(1)}, u32[]{:S(2)}) copy-start(f32[4,26,1024]{2,1,0:T(8,128)S(1)} %get-tuple-element.24) | copy-start | bytes 1277956
  45.6 8.1 %copy-start.13 = (f32[4,26,1024]{2,1,0:T(8,128)}, f32[4,26,1024]{2,1,0:T(8,128)S(1)}, u32[]{:S(2)}) copy-start(f32[4,26,1024]{2,1,0:T(8,128)S(1)} %get-tuple-element.40) | copy-start | bytes 1277956
  45.6 11.3 %copy-start = (f32[4,26,1024]{2,1,0:T(8,128)}, f32[4,26,1024]{2,1,0:T(8,128)S(1)}, u32[]{:S(2)}) copy-start(f32[4,26,1024]{2,1,0:T(8,128)S(1)} %get-tuple-element.33) | copy-start | bytes 1277956
  45.6 11.3 %copy-start.2 = (f32[4,26,1024]{2,1,0:T(8,128)}, f32[4,26,1024]{2,1,0:T(8,128)S(1)}, u32[]{:S(2)}) copy-start(f32[4,26,1024]{2,1,0:T(8,128)S(1)} %get-tuple-element.25) | copy-start | bytes 1277956
  45.6 11.3 %copy-start.4 = (f32[4,26,1024]{2,1,0:T(8,128)}, f32[4,26,1024]{2,1,0:T(8,128)S(1)}, u32[]{:S(2)}) copy-start(f32[4,26,1024]{2,1,0:T(8,128)S(1)} %get-tuple-element.41) | copy-start | bytes 1277956
  45.6 2.6 %copy-start.18 = (f32[4,1,26,1024]{3,2,0,1:T(8,128)S(1)}, f32[4,1,26,1024]{3,2,0,1:T(8,128)}, u32[]{:S(2)}) copy-start(f32[4,1,26,1024]{3,2,0,1:T(8,128)} %reshape.97) | copy-start | bytes 1277956
  64.5 19.4 %copy-start.22 = (f32[4,32]{1,0:T(4,128)S(1)}, f32[4,32]{1,0:T(4,128)}, u32[]{:S(2)}) copy-start(f32[4,32]{1,0:T(4,128)} %param.14) | copy-start | bytes 1540
  124.9 2.6 %copy-start.5 = (f32[4,26,1024]{2,1,0:T(8,128)S(1)}, f32[4,26,1024]{2,1,0:T(8,128)}, u32[]{:S(2)}) copy-start(f32[4,26,1024]{2,1,0:T(8,128)} %copy-done.4) | copy-start | bytes 1277956
  124.9 2.6 %copy-start.16 = (f32[4,26,1024]{2,1,0:T(8,128)S(1)}, f32[4,26,1024]{2,1,0:T(8,128)}, u32[]{:S(2)}) copy-start(f32[4,26,1024]{2,1,0:T(8,128)} %copy-done.15) | copy-start | bytes 1277956
  127.5 2.8 %copy-start.14 = (f32[4,26,1024]{2,1,0:T(8,128)S(1)}, f32[4,26,1024]{2,1,0:T(8,128)}, u32[]{:S(2)}) copy-start(f32[4,26,1024]{2,1,0:T(8,128)} %copy-done.13) | copy-start | bytes 1277956
  130.3 3.2 %copy-start.10 = (f32[4,4,16,1024]{3,2,1,0:T(8,128)S(1)}, f32[4,4,16,1024]{3,2,1,0:T(8,128)}, u32[]{:S(2)}) copy-start(f32[4,4,16,1024]{3,2,1,0:T(8,128)} %param.10) | copy-start | bytes 3145732
  130.3 3.2 %copy-start.12 = (f32[4,26,1024]{2,1,0:T(8,128)S(1)}, f32[4,26,1024]{2,1,0:T(8,128)}, u32[]{:S(2)}) copy-start(f32[4,26,1024]{2,1,0:T(8,128)} %copy-done.11) | copy-start | bytes 1277956
  133.5 5.2 %copy-start.17 = (f32[4,4,16,1024]{3,2,0,1:T(8,128)S(1)}, f32[4,4,16,1024]{3,2,0,1:T(8,128)}, u32[]{:S(2)}) copy-start(f32[4,4,16,1024]{3,2,0,1:T(8,128)} %slice.345) | copy-start | bytes 3145732
  (7 other events, 12.4 us)
Sparse Core Ops, SparseCore 0:
  142.8 36.7 all-reduce.33
where the time goes:
time: 189 us; the launch traced here: 188 us
  other arithmetic  72.2 us (38%)
  waiting for transfers between devices  36.9 us (20%)
  blocking collectives  32.1 us (17%)
  local copies, waits for them, and re-layouts  17.7 us (9%)
  starting transfers between devices  15 us (8%)
  between operations  14 us (7%)
    psum x1, waiting for transfers between devices, per_device(): summed = lax.psum(local_terms, 'src')  36.9 us
    scatter-add x2, other arithmetic, surface_source(): plane = jnp.zeros((sources_here, span * columns), jnp.float32).at[source_...  36.7 us
    psum x1, blocking collectives, per_device(): predicted = lax.psum(local_readings, 'space')  16.1 us
    all_gather x1, blocking collectives, per_device(): whole_sigma = lax.all_gather(conductivity, 'src', axis=2, tiled=True)  16 us
    add x4, other arithmetic, chebyshev(): factor_next * factor * direction  11.9 us
    ppermute x3, starting transfers between devices, padded_2(): lax.ppermute(lax.slice_in_dim(block, block.shape[dim] - width, None, axis...  11.1 us
    add x2, other arithmetic, chebyshev(): potential = potential + direction  9.93 us
    div x2, other arithmetic, chebyshev(): direction = inverse * residual / THETA  5.15 us
  transfers between devices with their start and end apart: 7, of which 1 were waited for; matrix products, arithmetic and copies ran while one was open for 36% of the time, Pallas kernels for 0%

commit v1 on v0

--- a/solution.py
+++ b/solution.py
@@ -185,7 +185,9 @@
     forward_pad = forward[:, :, margin_rows - 1 : margin_rows + row_count + 1, :]
     adjoint_pad = adjoint[:, :, margin_rows - 1 : margin_rows + row_count + 1, :]
     local_terms = jnp.sum(sensitivity(forward_pad, adjoint_pad), axis=0)
-    summed = lax.psum(local_terms, "src")
+    summed = local_terms
+    for hop in (1, 2):
+        summed = summed + lax.ppermute(summed, "src", [(dev, dev ^ hop) for dev in range(4)])
     share = columns // lax.axis_size("src")
     return lax.dynamic_slice_in_dim(summed, lax.axis_index("src") * share, share, 2)
 

time: 189 us -> 157 us (0.83)
  waiting for transfers between devices: 36.9 us -> 14.6 us
  between operations: 14 us -> 0.58 us
  starting transfers between devices: 15 us -> 19.5 us
    psum x1 -> x0, waiting for transfers between devices: 36.9 us -> none  [per_device(): summed = lax.psum(local_terms, 'src')]
    ppermute x0 -> x2, waiting for transfers between devices: none -> 14.6 us  [per_device(): lax.ppermute(summed, 'src', [(dev, dev ^ hop) for dev in range(4)])]
    ppermute x0 -> x2, starting transfers between devices: none -> 4.46 us  [per_device(): lax.ppermute(summed, 'src', [(dev, dev ^ hop) for dev in range(4)])]
  transfers between devices with their start and end apart: 7 -> 8, of which waited for: 1 -> 2; matrix products, arithmetic and copies ran while one was open for 36% -> 43% of each run, Pallas kernels for 0% -> 0%
where the time goes in v1:
time: 157 us; the launch traced here: 156 us
  other arithmetic  72.7 us (46%)
  blocking collectives  32.1 us (20%)
  starting transfers between devices  19.5 us (12%)
  local copies, waits for them, and re-layouts  16.3 us (10%)
  waiting for transfers between devices  14.6 us (9%)
    scatter-add x2, other arithmetic, surface_source(): plane = jnp.zeros((sources_here, span * columns), jnp.float32).at[source_...  37.3 us
    psum x1, blocking collectives, per_device(): predicted = lax.psum(local_readings, 'space')  16.1 us
    all_gather x1, blocking collectives, per_device(): whole_sigma = lax.all_gather(conductivity, 'src', axis=2, tiled=True)  16 us
    ppermute x2, waiting for transfers between devices, per_device(): lax.ppermute(summed, 'src', [(dev, dev ^ hop) for dev in range(4)])  14.6 us
    add x4, other arithmetic, chebyshev(): factor_next * factor * direction  11.8 us
    ppermute x3, starting transfers between devices, padded_2(): lax.ppermute(lax.slice_in_dim(block, block.shape[dim] - width, None, axis...  11.1 us
    add x2, other arithmetic, chebyshev(): potential = potential + direction  9.88 us
    div x2, other arithmetic, chebyshev(): direction = inverse * residual / THETA  5.1 us
  transfers between devices with their start and end apart: 8, of which 2 were waited for; matrix products, arithmetic and copies ran while one was open for 43% of the time, Pallas kernels for 0%

profile of v1, /device:TPU:0, one launch (start us, length us, event | category | flops | bytes accessed | tf_op | source)
XLA Modules:
  0.0 155.7 jit_solution(9272554581398346421)
XLA Ops:
  0.0 16.0 %all_gather.3 = f32[4,16,1024]{2,1,0:T(8,128)S(1)} all-gather(f32[4,16,256]{2,1,0:T(8,128)} %param.11), channel_id=1, replica_groups=mesh['space'=8,'src'=4] {'src'}, dimensions={2}, use_global_device_ids=true | all-gather | bytes 327680 | tf_op jit(solution)/shard_map/all_gather | solution.py:137
  18.6 2.3 %fusion.150 = (f32[4,4,5,1024]{3,2,0,1:T(8,128)}, f32[4,4,5,1024]{3,2,0,1:T(8,128)}) fusion(f32[4,4,16,1024]{3,2,1,0:T(8,128)} %param.9), kind=kLoop, calls=%fused_computation.234 | loop fusion | bytes 1703936 | tf_op jit(solution)/shard_map/slice | solution.py:20
  20.9 5.6 %collective-permute-start = (f32[4,4,5,1024]{3,2,0,1:T(8,128)}, f32[4,4,5,1024]{3,2,0,1:T(8,128)}, u32[]{:S(2)}, u32[]{:S(2)}) collective-permute-start(f32[4,4,5,1024]{3,2,0,1:T(8,128)} %get-tuple-element.28), channel_id=1, source_target_pairs={{0,4},{4,8},{8,12},{12,16},{16,20},{20,24},{24,28},{1,5},{5,9},{9,... | collective-permute-start | bytes 983048 | tf_op jit(solution)/shard_map/ppermute | solution.py:19
  28.9 4.3 %collective-permute-start.4 = (f32[4,4,5,1024]{3,2,0,1:T(8,128)}, f32[4,4,5,1024]{3,2,0,1:T(8,128)}, u32[]{:S(2)}, u32[]{:S(2)}) collective-permute-start(f32[4,4,5,1024]{3,2,0,1:T(8,128)} %get-tuple-element.26), channel_id=1, source_target_pairs={{0,4},{4,8},{8,12},{12,16},{16,20},{20,24},{24,28},{1,5},{5,9},{9,... | collective-permute-start | bytes 983048 | tf_op jit(solution)/shard_map/ppermute | solution.py:19
  39.5 2.2 %pad_maximum_fusion = f32[4,4,26,1024]{3,2,0,1:T(8,128)S(1)} fusion(f32[4,4,5,1024]{3,2,0,1:T(8,128)} %collective-permute-done.1, f32[4,4,5,1024]{3,2,0,1:T(8,128)} %collective-permute-done, f32[4,4,16,1024]{3,2,1,0:T(8,128)S(1)} %copy-done.8), kind=kLoop, calls=%fused_computation.130 | loop fusion | flops 851968 | bytes 3407872 | tf_op jit(solution)/shard_map/concatenate | solution.py:23
  41.8 2.5 %multiply_multiply_fusion.1 = (f32[4,4,26,1024]{3,2,0,1:T(8,128)S(1)}, f32[4,4,26,1024]{3,2,0,1:T(8,128)S(1)}) fusion(f32[4,26,1024]{2,1,0:T(8,128)S(1)} %get-tuple-element.15, f32[26]{0:T(128)S(1)} %and_convert_fusion, f32[4,26,1024]{2,1,0:T(8,128)S(1)} %get-tuple-element.31, f32[4,4,26,1024]{3,2,0,1:T(8,128)S(1)} %pad_maximum_fusion, ...), kind=kLoop, calls=%fused_computation.137 | loop fusion | flops 7241728 | bytes 8945768 | tf_op jit(solution)/shard_map/div | solution.py:75
  44.3 2.7 %multiply_add_fusion.3 = (f32[4,4,26,1024]{3,2,0,1:T(8,128)S(1)}, f32[4,4,26,1024]{3,2,0,1:T(8,128)S(1)}) fusion(f32[4,4,26,1024]{3,2,0,1:T(8,128)S(1)} %get-tuple-element.23, f32[4,26,1024]{2,1,0:T(8,128)S(1)} %get-tuple-element.41, f32[4,26,1024]{2,1,0:T(8,128)S(1)} %get-tuple-element.15, f32[26]{0:T(128)S(1)} %and_convert_fusion, ...), kind=kLoop, calls=%fused_computation.135 | loop fusion | flops 8093696 | bytes 10649704 | tf_op jit(solution)/shard_map/add | solution.py:85
  47.1 3.2 %multiply_add_fusion.2 = (f32[4,4,26,1024]{3,2,0,1:T(8,128)S(1)}, f32[4,4,26,1024]{3,2,0,1:T(8,128)S(1)}) fusion(f32[4,26,1024]{2,1,0:T(8,128)S(1)} %get-tuple-element.40, f32[4,4,26,1024]{3,2,0,1:T(8,128)S(1)} %get-tuple-element.21, f32[4,26,1024]{2,1,0:T(8,128)S(1)} %get-tuple-element.41, f32[4,4,26,1024]{3,2,0,1:T(8,128)S(1)} %get-tuple-element.23, ...), kind=kLoop, calls=%fused_computation.134 | loop fusion | flops 9371648 | bytes 12779624 | tf_op jit(solution)/shard_map/add | solution.py:85
  50.3 4.9 %fusion.37 = f32[4,4,26,1024]{3,2,0,1:T(8,128)S(1)} fusion(f32[4,4,26,1024]{3,2,0,1:T(8,128)S(1)} %get-tuple-element.19, f32[4,4,26,1024]{3,2,0,1:T(8,128)S(1)} %get-tuple-element.18, f32[4,4,26,1024]{3,2,0,1:T(8,128)S(1)} %get-tuple-element.23, f32[4,26,1024]{2,1,0:T(8,128)S(1)} %get-tuple-element.14, f32[26]{0:T(128)S(1)} %and_convert_fusion, ...), kind=kLoop, calls=%fused_computation.73 | loop fusion | flops 12353536 | bytes 14483560 | tf_op jit(solution)/shard_map/add | solution.py:79
  57.9 1.5 gather_fusion
  59.5 1.5 gather_fusion.1
  61.2 16.1 %psum.7 = f32[4,32]{1,0:T(4,128)S(1)} all-reduce(f32[4,32]{1,0:T(4,128)S(1)} %fusion.136), channel_id=1, replica_groups=mesh['space'=8,'src'=4] {'space'}, use_global_device_ids=true, to_apply=%region_1.3 | all-reduce | flops 128 | bytes 1024 | tf_op jit(solution)/shard_map/psum | solution.py:172
  78.2 36.5 %scatter_fusion.1 = f32[4,26624]{1,0:T(4,128)} fusion(f32[4,26624]{1,0:T(4,128)} %broadcast.247, s32[256]{0:T(256)S(1)} %reshape.118, f32[256]{0:T(256)S(1)} %reshape.120), kind=kCustom, calls=%fused_computation.3 | custom fusion | flops 256 | bytes 5120 | tf_op jit(solution)/shard_map/scatter-add | solution.py:127
  114.7 2.2 %reshape.98 = f32[4,1,26,1024]{3,2,0,1:T(8,128)} reshape(f32[4,26624]{1,0:T(4,128)} %scatter_fusion.1) | data formatting | bytes 851968 | tf_op jit(solution)/shard_map/reshape | solution.py:129
  116.9 2.0 %pad_maximum_fusion.1 = f32[4,4,26,1024]{3,2,0,1:T(8,128)S(1)} fusion(f32[4,4,5,1024]{3,2,0,1:T(8,128)} %collective-permute-done.5, f32[4,4,5,1024]{3,2,0,1:T(8,128)} %collective-permute-done.4, f32[4,4,16,1024]{3,2,1,0:T(8,128)} %param.10), kind=kLoop, calls=%fused_computation.131 | loop fusion | flops 851968 | bytes 3407872 | tf_op jit(solution)/shard_map/concatenate | solution.py:23
  118.9 2.6 %multiply_multiply_fusion = (f32[4,4,26,1024]{3,2,0,1:T(8,128)S(1)}, f32[4,4,26,1024]{3,2,0,1:T(8,128)S(1)}) fusion(f32[4,26,1024]{2,1,0:T(8,128)S(1)} %get-tuple-element.15, f32[26]{0:T(128)S(1)} %and_convert_fusion, f32[4,26,1024]{2,1,0:T(8,128)S(1)} %get-tuple-element.31, f32[4,4,26,1024]{3,2,0,1:T(8,128)S(1)} %pad_maximum_fusion.1, ...), kind=kLoop, calls=%fused_computation.136 | loop fusion | flops 7241728 | bytes 8945768 | tf_op jit(solution)/shard_map/div | solution.py:75
  121.5 2.7 %multiply_add_fusion.1 = (f32[4,4,26,1024]{3,2,0,1:T(8,128)S(1)}, f32[4,4,26,1024]{3,2,0,1:T(8,128)S(1)}) fusion(f32[4,4,26,1024]{3,2,0,1:T(8,128)S(1)} %get-tuple-element.11, f32[4,26,1024]{2,1,0:T(8,128)S(1)} %copy-done.5, f32[4,26,1024]{2,1,0:T(8,128)S(1)} %get-tuple-element.15, f32[26]{0:T(128)S(1)} %and_convert_fusion, ...), kind=kLoop, calls=%fused_computation.133 | loop fusion | flops 8093696 | bytes 10649704 | tf_op jit(solution)/shard_map/add | solution.py:85
  124.3 3.2 %multiply_add_fusion = (f32[4,4,26,1024]{3,2,0,1:T(8,128)S(1)}, f32[4,4,26,1024]{3,2,0,1:T(8,128)S(1)}) fusion(f32[4,26,1024]{2,1,0:T(8,128)S(1)} %copy-done.14, f32[4,4,26,1024]{3,2,0,1:T(8,128)S(1)} %get-tuple-element.9, f32[4,26,1024]{2,1,0:T(8,128)S(1)} %copy-done.5, f32[4,4,26,1024]{3,2,0,1:T(8,128)S(1)} %get-tuple-element.11, ...), kind=kLoop, calls=%fused_computation.132 | loop fusion | flops 9371648 | bytes 12779624 | tf_op jit(solution)/shard_map/add | solution.py:85
  127.5 5.0 %fusion.76 = f32[4,4,26,1024]{3,2,0,1:T(8,128)S(1)} fusion(f32[4,4,26,1024]{3,2,0,1:T(8,128)S(1)} %get-tuple-element.7, f32[4,4,26,1024]{3,2,0,1:T(8,128)S(1)} %get-tuple-element.6, f32[4,4,26,1024]{3,2,0,1:T(8,128)S(1)} %get-tuple-element.11, f32[4,26,1024]{2,1,0:T(8,128)S(1)} %copy-done.12, f32[26]{0:T(128)S(1)} %and_convert_fusion, ...), kind=kLoop, calls=%fused_computation.112 | loop fusion | flops 12353536 | bytes 14483560 | tf_op jit(solution)/shard_map/add | solution.py:79
  134.1 1.8 %fusion.101 = f32[4,16,1024]{2,1,0:T(8,128)S(1)} fusion(f32[4,4,16,1024]{3,2,0,1:T(8,128)S(1)} %copy-done.17, f32[4,4,16,1024]{3,2,0,1:T(8,128)S(1)} %slice.349, f32[4,4,26,1024]{3,2,0,1:T(8,128)S(1)} %fusion.76, f32[4,4,26,1024]{3,2,0,1:T(8,128)S(1)} %copy-done.7), kind=kLoop, calls=%fused_computation.153 | loop fusion | flops 8585216 | bytes 6553600 | tf_op jit(solution)/shard_map/reduce_sum | solution.py:187
  136.0 1.6 %collective-permute-start.6 = (f32[4,16,1024]{2,1,0:T(8,128)S(1)}, f32[4,16,1024]{2,1,0:T(8,128)S(1)}, u32[]{:S(2)}, u32[]{:S(2)}) collective-permute-start(f32[4,16,1024]{2,1,0:T(8,128)S(1)} %neg.7), channel_id=1, source_target_pairs={{0,1},{1,0},{2,3},{3,2},{4,5},{5,4},{6,7},{7,6},{8,9},{9,8},{10,11... | collective-permute-start | bytes 786440 | tf_op jit(solution)/shard_map/ppermute | solution.py:190
  137.5 4.9 %collective-permute-done.6 = f32[4,16,1024]{2,1,0:T(8,128)S(1)} collective-permute-done((f32[4,16,1024]{2,1,0:T(8,128)S(1)}, f32[4,16,1024]{2,1,0:T(8,128)S(1)}, u32[]{:S(2)}, u32[]{:S(2)}) %collective-permute-start.6) | collective-permute-done | bytes 262176 | tf_op jit(solution)/shard_map/ppermute | solution.py:190
  142.4 2.9 %collective-permute-start.7 = (f32[4,16,1024]{2,1,0:T(8,128)S(1)}, f32[4,16,1024]{2,1,0:T(8,128)S(1)}, u32[]{:S(2)}, u32[]{:S(2)}) collective-permute-start(f32[4,16,1024]{2,1,0:T(8,128)S(1)} %negate_add_fusion), channel_id=1, source_target_pairs={{0,2},{1,3},{2,0},{3,1},{4,6},{5,7},{6,4},{7,5},{8,10},{9,11},{10,... | collective-permute-start | bytes 786440 | tf_op jit(solution)/shard_map/ppermute | solution.py:190
  145.3 9.7 %collective-permute-done.7 = f32[4,16,1024]{2,1,0:T(8,128)S(1)} collective-permute-done((f32[4,16,1024]{2,1,0:T(8,128)S(1)}, f32[4,16,1024]{2,1,0:T(8,128)S(1)}, u32[]{:S(2)}, u32[]{:S(2)}) %collective-permute-start.7) | collective-permute-done | bytes 262176 | tf_op jit(solution)/shard_map/ppermute | solution.py:190
  (95 shorter events, 17.3 us)
Async XLA Ops:
  0.0 27.8 %copy-start.9 = (f32[4,4,16,1024]{3,2,1,0:T(8,128)S(1)}, f32[4,4,16,1024]{3,2,1,0:T(8,128)}, u32[]{:S(2)}) copy-start(f32[4,4,16,1024]{3,2,1,0:T(8,128)} %param.10) | copy-start | bytes 3145732
  16.0 20.1 %collective-permute-start.2 = (f32[4,6,1024]{2,1,0:T(8,128)S(1)}, f32[4,6,1024]{2,1,0:T(8,128)S(1)}, u32[]{:S(2)}, u32[]{:S(2)}) collective-permute-start(f32[4,6,1024]{2,1,0:T(8,128)S(1)} %get-tuple-element.36), channel_id=1, source_target_pairs={{0,4},{4,8},{8,12},{12,16},{16,20},{20,24},{24,28},{1,5},{5,9},{9,... | collective-permute-start | bytes 294920 | tf_op jit(solution)/shard_map/ppermute | solution.py:19
  17.3 15.9 %copy-start.20 = (s32[4,2]{0,1:T(2,128)S(1)}, s32[4,2]{0,1:T(2,128)}, u32[]{:S(2)}) copy-start(s32[4,2]{0,1:T(2,128)} %param.12) | copy-start | bytes 100
  17.3 16.1 %copy-start.23 = (f32[2]{0:T(128)S(1)}, f32[2]{0:T(128)}, u32[]{:S(2)}) copy-start(f32[2]{0:T(128)} %constant.30.clone) | copy-start | bytes 28
  17.3 20.1 %collective-permute-start.3 = (f32[4,6,1024]{2,1,0:T(8,128)S(1)}, f32[4,6,1024]{2,1,0:T(8,128)S(1)}, u32[]{:S(2)}, u32[]{:S(2)}) collective-permute-start(f32[4,6,1024]{2,1,0:T(8,128)S(1)} %get-tuple-element.37), channel_id=1, source_target_pairs={{4,0},{8,4},{12,8},{16,12},{20,16},{24,20},{28,24},{5,1},{9,5},{13... | collective-permute-start | bytes 294920 | tf_op jit(solution)/shard_map/ppermute | solution.py:22
  20.9 18.2 %collective-permute-start = (f32[4,4,5,1024]{3,2,0,1:T(8,128)}, f32[4,4,5,1024]{3,2,0,1:T(8,128)}, u32[]{:S(2)}, u32[]{:S(2)}) collective-permute-start(f32[4,4,5,1024]{3,2,0,1:T(8,128)} %get-tuple-element.28), channel_id=1, source_target_pairs={{0,4},{4,8},{8,12},{12,16},{16,20},{20,24},{24,28},{1,5},{5,9},{9,... | collective-permute-start | bytes 983048 | tf_op jit(solution)/shard_map/ppermute | solution.py:19
  26.5 12.6 %collective-permute-start.1 = (f32[4,4,5,1024]{3,2,0,1:T(8,128)}, f32[4,4,5,1024]{3,2,0,1:T(8,128)}, u32[]{:S(2)}, u32[]{:S(2)}) collective-permute-start(f32[4,4,5,1024]{3,2,0,1:T(8,128)} %get-tuple-element.29), channel_id=1, source_target_pairs={{4,0},{8,4},{12,8},{16,12},{20,16},{24,20},{28,24},{5,1},{9,5},{13... | collective-permute-start | bytes 983048 | tf_op jit(solution)/shard_map/ppermute | solution.py:22
  28.9 88.0 %collective-permute-start.4 = (f32[4,4,5,1024]{3,2,0,1:T(8,128)}, f32[4,4,5,1024]{3,2,0,1:T(8,128)}, u32[]{:S(2)}, u32[]{:S(2)}) collective-permute-start(f32[4,4,5,1024]{3,2,0,1:T(8,128)} %get-tuple-element.26), channel_id=1, source_target_pairs={{0,4},{4,8},{8,12},{12,16},{16,20},{20,24},{24,28},{1,5},{5,9},{9,... | collective-permute-start | bytes 983048 | tf_op jit(solution)/shard_map/ppermute | solution.py:19
  36.1 80.8 %collective-permute-start.5 = (f32[4,4,5,1024]{3,2,0,1:T(8,128)}, f32[4,4,5,1024]{3,2,0,1:T(8,128)}, u32[]{:S(2)}, u32[]{:S(2)}) collective-permute-start(f32[4,4,5,1024]{3,2,0,1:T(8,128)} %get-tuple-element.27), channel_id=1, source_target_pairs={{4,0},{8,4},{12,8},{16,12},{20,16},{24,20},{28,24},{5,1},{9,5},{13... | collective-permute-start | bytes 983048 | tf_op jit(solution)/shard_map/ppermute | solution.py:22
  38.1 12.2 %copy-start.11 = (f32[4,26,1024]{2,1,0:T(8,128)}, f32[4,26,1024]{2,1,0:T(8,128)S(1)}, u32[]{:S(2)}) copy-start(f32[4,26,1024]{2,1,0:T(8,128)S(1)} %get-tuple-element.14) | copy-start | bytes 1277956
  39.1 5.3 %copy-start.15 = (f32[4,26,1024]{2,1,0:T(8,128)}, f32[4,26,1024]{2,1,0:T(8,128)S(1)}, u32[]{:S(2)}) copy-start(f32[4,26,1024]{2,1,0:T(8,128)S(1)} %get-tuple-element.24) | copy-start | bytes 1277956
  39.1 8.0 %copy-start.13 = (f32[4,26,1024]{2,1,0:T(8,128)}, f32[4,26,1024]{2,1,0:T(8,128)S(1)}, u32[]{:S(2)}) copy-start(f32[4,26,1024]{2,1,0:T(8,128)S(1)} %get-tuple-element.40) | copy-start | bytes 1277956
  39.1 11.2 %copy-start = (f32[4,26,1024]{2,1,0:T(8,128)}, f32[4,26,1024]{2,1,0:T(8,128)S(1)}, u32[]{:S(2)}) copy-start(f32[4,26,1024]{2,1,0:T(8,128)S(1)} %get-tuple-element.33) | copy-start | bytes 1277956
  39.1 11.2 %copy-start.2 = (f32[4,26,1024]{2,1,0:T(8,128)}, f32[4,26,1024]{2,1,0:T(8,128)S(1)}, u32[]{:S(2)}) copy-start(f32[4,26,1024]{2,1,0:T(8,128)S(1)} %get-tuple-element.25) | copy-start | bytes 1277956
  39.1 11.2 %copy-start.4 = (f32[4,26,1024]{2,1,0:T(8,128)}, f32[4,26,1024]{2,1,0:T(8,128)S(1)}, u32[]{:S(2)}) copy-start(f32[4,26,1024]{2,1,0:T(8,128)S(1)} %get-tuple-element.41) | copy-start | bytes 1277956
  39.1 2.6 %copy-start.18 = (f32[4,1,26,1024]{3,2,0,1:T(8,128)S(1)}, f32[4,1,26,1024]{3,2,0,1:T(8,128)}, u32[]{:S(2)}) copy-start(f32[4,1,26,1024]{3,2,0,1:T(8,128)} %reshape.97) | copy-start | bytes 1277956
  57.9 19.4 %copy-start.22 = (f32[4,32]{1,0:T(4,128)S(1)}, f32[4,32]{1,0:T(4,128)}, u32[]{:S(2)}) copy-start(f32[4,32]{1,0:T(4,128)} %param.14) | copy-start | bytes 1540
  118.9 2.6 %copy-start.5 = (f32[4,26,1024]{2,1,0:T(8,128)S(1)}, f32[4,26,1024]{2,1,0:T(8,128)}, u32[]{:S(2)}) copy-start(f32[4,26,1024]{2,1,0:T(8,128)} %copy-done.4) | copy-start | bytes 1277956
  121.5 2.8 %copy-start.14 = (f32[4,26,1024]{2,1,0:T(8,128)S(1)}, f32[4,26,1024]{2,1,0:T(8,128)}, u32[]{:S(2)}) copy-start(f32[4,26,1024]{2,1,0:T(8,128)} %copy-done.13) | copy-start | bytes 1277956
  124.3 3.2 %copy-start.10 = (f32[4,4,16,1024]{3,2,1,0:T(8,128)S(1)}, f32[4,4,16,1024]{3,2,1,0:T(8,128)}, u32[]{:S(2)}) copy-start(f32[4,4,16,1024]{3,2,1,0:T(8,128)} %param.10) | copy-start | bytes 3145732
  124.3 3.2 %copy-start.12 = (f32[4,26,1024]{2,1,0:T(8,128)S(1)}, f32[4,26,1024]{2,1,0:T(8,128)}, u32[]{:S(2)}) copy-start(f32[4,26,1024]{2,1,0:T(8,128)} %copy-done.11) | copy-start | bytes 1277956
  127.5 5.2 %copy-start.17 = (f32[4,4,16,1024]{3,2,0,1:T(8,128)S(1)}, f32[4,4,16,1024]{3,2,0,1:T(8,128)}, u32[]{:S(2)}) copy-start(f32[4,4,16,1024]{3,2,0,1:T(8,128)} %slice.345) | copy-start | bytes 3145732
  136.0 6.4 %collective-permute-start.6 = (f32[4,16,1024]{2,1,0:T(8,128)S(1)}, f32[4,16,1024]{2,1,0:T(8,128)S(1)}, u32[]{:S(2)}, u32[]{:S(2)}) collective-permute-start(f32[4,16,1024]{2,1,0:T(8,128)S(1)} %neg.7), channel_id=1, source_target_pairs={{0,1},{1,0},{2,3},{3,2},{4,5},{5,4},{6,7},{7,6},{8,9},{9,8},{10,11... | collective-permute-start | bytes 786440 | tf_op jit(solution)/shard_map/ppermute | solution.py:190
  142.4 12.6 %collective-permute-start.7 = (f32[4,16,1024]{2,1,0:T(8,128)S(1)}, f32[4,16,1024]{2,1,0:T(8,128)S(1)}, u32[]{:S(2)}, u32[]{:S(2)}) collective-permute-start(f32[4,16,1024]{2,1,0:T(8,128)S(1)} %negate_add_fusion), channel_id=1, source_target_pairs={{0,2},{1,3},{2,0},{3,1},{4,6},{5,7},{6,4},{7,5},{8,10},{9,11},{10,... | collective-permute-start | bytes 786440 | tf_op jit(solution)/shard_map/ppermute | solution.py:190
  (8 other events, 15.0 us)
